TPU v7x, 32 devices: a whole 2x2x4 slice. The times are simulated.
32 devices in a mesh: groups: 2 (over x), spatial: 16 (over z, y, core).
Axes of the slice: x: 2, y: 2, z: 4, core: 2. Of those that a mesh axis runs over, the one named last changes fastest.
Arguments:
- fields: bfloat16 [1024, 128, 768], P(('groups', 'spatial')), parts along dimension 0, may hold values from -6 to 6
- norm1_gain: float32 [768], replicated, may hold values from 0.5 to 1.5
- norm1_bias: float32 [768], replicated, may hold values from -3 to 3
- spectral_w1: float32 [2, 8, 96, 96], replicated, may hold values from -0.4375 to 0.4375
- spectral_b1: float32 [2, 8, 96], replicated, may hold values from -3 to 3
- spectral_w2: float32 [2, 8, 96, 96], replicated, may hold values from -0.4375 to 0.4375
- spectral_b2: float32 [2, 8, 96], replicated, may hold values from -3 to 3
- norm2_gain: float32 [768], replicated, may hold values from 0.5 to 1.5
- norm2_bias: float32 [768], replicated, may hold values from -3 to 3
- fc1_weight: bfloat16 [768, 3072], replicated, may hold values from -0.21875 to 0.21875
- fc1_bias: float32 [3072], replicated, may hold values from -3 to 3
- fc2_weight: bfloat16 [3072, 768], replicated, may hold values from -0.109375 to 0.109375
- fc2_bias: float32 [768], replicated, may hold values from -3 to 3
Outputs:
- next_state: bfloat16 [1024, 128, 768], P(('groups', 'spatial')), parts along dimension 0
- anomaly: bfloat16 [1024, 128, 768], P(('groups', 'spatial')), parts along dimension 0
There are 2 independent parts, one for each index of `groups`. A program takes and returns all parts, laid end to end along the dimension named above; an argument that names none is the same for every part. Nothing has to cross between parts.
All inputs are finite; a program needn't handle non-finite values.
Results may differ from a plain program's by a relative error of at most 0.0056.
Values may be sent and summed in bfloat16 or wider, within the bound.
A program may use at most 192 MiB of HBM per device.

v0:
```python
import math
import jax
import jax.numpy as jnp
from jax import lax
from jax.sharding import Mesh, PartitionSpec as P

MEMBERS = 8
EPSILON = 1e-06
SHRINK = 0.01
FULL_PRECISION = lax.Precision.HIGHEST


def from_behind(block, axis, distance):
    devices = range(lax.axis_size(axis))
    route = [((i - distance) % len(devices), i) for i in devices]
    return lax.ppermute(block, axis, route)


def layer_norm(values, gain, offset_term):
    center = values - jnp.mean(values, axis=-1, keepdims=True)
    spread = jnp.mean(center * center, axis=-1, keepdims=True)
    return center * lax.rsqrt(spread + EPSILON) * gain + offset_term


def soft_shrink(values):
    return jnp.where(
        values > SHRINK, values - SHRINK, jnp.where(values < -SHRINK, values + SHRINK, 0.0)
    )


def contract(form, left, right):
    return jnp.einsum(form, left, right, precision=FULL_PRECISION)


def block_product(values, weight):
    return jnp.einsum("...bi,bio->...bo", values, weight, precision=FULL_PRECISION)


def angle_table(first_len, second_len, modulus):
    first_index = lax.broadcasted_iota(jnp.int32, (first_len, second_len), 0)
    second_index = lax.broadcasted_iota(jnp.int32, (first_len, second_len), 1)
    phase = first_index * second_index % modulus
    return phase.astype(jnp.float32) * (2.0 * math.pi / modulus)


def spectral_layer(real_part, imag_part, w_first, b_first, w_second, b_second):
    shape = real_part.shape
    block_count = w_first.shape[1]
    split_shape = shape[:-1] + (block_count, shape[-1] // block_count)
    real_part = real_part.reshape(split_shape)
    imag_part = imag_part.reshape(split_shape)
    hidden_real = jax.nn.relu(
        block_product(real_part, w_first[0]) - block_product(imag_part, w_first[1]) + b_first[0]
    )
    hidden_imag = jax.nn.relu(
        block_product(imag_part, w_first[0]) + block_product(real_part, w_first[1]) + b_first[1]
    )
    mixed_real = (
        block_product(hidden_real, w_second[0])
        - block_product(hidden_imag, w_second[1])
        + b_second[0]
    )
    mixed_imag = (
        block_product(hidden_imag, w_second[0])
        + block_product(hidden_real, w_second[1])
        + b_second[1]
    )
    return (soft_shrink(mixed_real).reshape(shape), soft_shrink(mixed_imag).reshape(shape))


def longitude_forward(normed, lon_len):
    angles = angle_table(lon_len, lon_len // 2, lon_len)
    factor = 1.0 / math.sqrt(lon_len)
    real_part = contract("rld,lk->rkd", normed, jnp.cos(angles) * factor)
    imag_part = -contract("rld,lk->rkd", normed, jnp.sin(angles) * factor)
    return (real_part, imag_part)


def longitude_inverse(real_part, imag_part, lon_len):
    half_len = lon_len // 2
    angles = angle_table(lon_len, half_len, lon_len)
    column_index = lax.broadcasted_iota(jnp.int32, (1, half_len), 1)
    weights = jnp.where(column_index == 0, 1.0, 2.0) / math.sqrt(lon_len)
    cosine_table = jnp.cos(angles) * weights
    sine_table = jnp.sin(angles) * weights
    return contract("rkd,lk->rld", real_part, cosine_table) - contract(
        "rkd,lk->rld", imag_part, sine_table
    )


def latitude_work(real_part, imag_part, w_first, b_first, w_second, b_second):
    member_rows, mode_count, channels = real_part.shape
    lat_len = member_rows // MEMBERS
    angles = angle_table(lat_len, lat_len, lat_len)
    factor = 1.0 / math.sqrt(lat_len)
    cosine_table = jnp.cos(angles) * factor
    sine_table = jnp.sin(angles) * factor
    grid_real = real_part.reshape(MEMBERS, lat_len, mode_count, channels)
    grid_imag = imag_part.reshape(MEMBERS, lat_len, mode_count, channels)
    spec_real = contract("qp,mpkd->mqkd", cosine_table, grid_real) + contract(
        "qp,mpkd->mqkd", sine_table, grid_imag
    )
    spec_imag = contract("qp,mpkd->mqkd", cosine_table, grid_imag) - contract(
        "qp,mpkd->mqkd", sine_table, grid_real
    )
    mixed_real, mixed_imag = spectral_layer(
        spec_real, spec_imag, w_first, b_first, w_second, b_second
    )
    back_real = contract("qp,mpkd->mqkd", cosine_table, mixed_real) - contract(
        "qp,mpkd->mqkd", sine_table, mixed_imag
    )
    back_imag = contract("qp,mpkd->mqkd", cosine_table, mixed_imag) + contract(
        "qp,mpkd->mqkd", sine_table, mixed_real
    )
    return (
        back_real.reshape(member_rows, mode_count, channels),
        back_imag.reshape(member_rows, mode_count, channels),
    )


def on_device(
    fields,
    norm1_gain,
    norm1_bias,
    spectral_w1,
    spectral_b1,
    spectral_w2,
    spectral_b2,
    norm2_gain,
    norm2_bias,
    fc1_weight,
    fc1_bias,
    fc2_weight,
    fc2_bias,
):
    row_count, lon_len, channels = fields.shape
    state = fields.astype(jnp.float32)
    normed = layer_norm(state, norm1_gain, norm1_bias)
    real_part, imag_part = longitude_forward(normed, lon_len)
    real_part, imag_part = (
        lax.all_to_all(real_part, "spatial", split_axis=1, concat_axis=0, tiled=True),
        lax.all_to_all(imag_part, "spatial", split_axis=1, concat_axis=0, tiled=True),
    )
    real_part, imag_part = latitude_work(
        real_part, imag_part, spectral_w1, spectral_b1, spectral_w2, spectral_b2
    )
    real_part, imag_part = (
        lax.all_to_all(real_part, "spatial", split_axis=0, concat_axis=1, tiled=True),
        lax.all_to_all(imag_part, "spatial", split_axis=0, concat_axis=1, tiled=True),
    )
    filtered = longitude_inverse(real_part, imag_part, lon_len)
    residual = (filtered + normed + state).reshape(row_count * lon_len, channels)
    normed2 = layer_norm(residual, norm2_gain, norm2_bias).astype(jnp.bfloat16)
    hidden = jax.nn.gelu(
        jnp.dot(normed2, fc1_weight, preferred_element_type=jnp.float32) + fc1_bias,
        approximate=False,
    ).astype(jnp.bfloat16)
    updated = residual + jnp.dot(hidden, fc2_weight, preferred_element_type=jnp.float32) + fc2_bias
    next_state = updated.astype(jnp.bfloat16).reshape(row_count, lon_len, channels)
    return next_state


def ensemble_step(next_state):
    state_values = next_state.astype(jnp.float32)
    summed = lax.psum(state_values, "member")
    anomaly = (state_values - summed / MEMBERS).astype(jnp.bfloat16)
    return (next_state, anomaly)


def solution(mesh):
    placed = (
        P(("groups", "spatial"), None, None),
        P(),
        P(),
        P(),
        P(),
        P(),
        P(),
        P(),
        P(),
        P(),
        P(),
        P(),
        P(),
    )
    update = jax.shard_map(
        on_device,
        mesh=mesh,
        in_specs=placed,
        out_specs=P(("groups", "spatial"), None, None),
        check_vma=False,
    )
    member_span = mesh.shape["spatial"] // MEMBERS
    ensemble_mesh = Mesh(
        mesh.devices.reshape(mesh.shape["groups"], MEMBERS, member_span),
        ("groups", "member", "half"),
    )
    member_rows = P(("groups", "member", "half"), None, None)
    spread = jax.shard_map(
        ensemble_step,
        mesh=ensemble_mesh,
        in_specs=(member_rows,),
        out_specs=(member_rows, member_rows),
        check_vma=False,
    )

    def step(*args):
        return spread(update(*args))

    return step
```

profile of v0, /device:TPU:0, one launch (start us, length us, event | category | flops | bytes accessed | tf_op | source)
XLA Modules:
  0.0 1506.0 jit_solution(8603126026089970054)
XLA Ops:
  31.3 12.0 fusion.94
  49.6 95.7 %all-to-all-done.1 = f32[32,64,768]{2,0,1:T(8,128)} async-done(((f32[32,64,768]{2,0,1:T(8,128)}), f32[32,64,768]{2,0,1:T(8,128)}, u32[]{:S(2)}, u32[]{:S(2)}) %all-to-all-start.1) | async-done | bytes 6291488 | tf_op jit(solution)/shard_map/all_to_all | solution.py:142
  145.3 28.5 %all-to-all-start = ((f32[32,64,768]{2,0,1:T(8,128)}), f32[32,64,768]{2,0,1:T(8,128)}, u32[]{:S(2)}, u32[]{:S(2)}) async-start(f32[32,64,768]{2,0,1:T(8,128)} %copy.57), calls=%async_computation | async-start | bytes 12582912 | tf_op jit(solution)/shard_map/all_to_all | solution.py:141
  193.1 94.8 %all-to-all-done = f32[32,64,768]{2,0,1:T(8,128)} async-done(((f32[32,64,768]{2,0,1:T(8,128)}), f32[32,64,768]{2,0,1:T(8,128)}, u32[]{:S(2)}, u32[]{:S(2)}) %all-to-all-start) | async-done | bytes 6291488 | tf_op jit(solution)/shard_map/all_to_all | solution.py:141
  302.2 9.9 reshape.102
  312.1 13.7 fusion.58
  325.9 9.9 fusion.60
  343.9 9.9 reshape.101
  353.8 13.1 add_maximum_fusion
  376.5 9.9 fusion.52
  396.0 14.9 select_bitcast_fusion
  410.9 10.9 copy.70
  431.5 12.2 select_bitcast_fusion.1
  443.7 10.9 copy.69
  488.4 28.2 %all-to-all-start.2 = ((f32[512,4,768]{2,1,0:T(4,128)}), f32[512,4,768]{2,1,0:T(4,128)}, u32[]{:S(2)}, u32[]{:S(2)}) async-start(f32[512,4,768]{2,1,0:T(4,128)} %copy.72), calls=%async_computation.2 | async-start | bytes 12582912 | tf_op jit(solution)/shard_map/all_to_all | solution.py:148
  539.2 91.6 %all-to-all-done.2 = f32[512,4,768]{2,1,0:T(4,128)} async-done(((f32[512,4,768]{2,1,0:T(4,128)}), f32[512,4,768]{2,1,0:T(4,128)}, u32[]{:S(2)}, u32[]{:S(2)}) %all-to-all-start.2) | async-done | bytes 6291488 | tf_op jit(solution)/shard_map/all_to_all | solution.py:148
  630.7 28.5 %all-to-all-start.3 = ((f32[512,4,768]{2,1,0:T(4,128)}), f32[512,4,768]{2,1,0:T(4,128)}, u32[]{:S(2)}, u32[]{:S(2)}) async-start(f32[512,4,768]{2,1,0:T(4,128)} %copy.76), calls=%async_computation.3 | async-start | bytes 12582912 | tf_op jit(solution)/shard_map/all_to_all | solution.py:149
  677.7 95.6 %all-to-all-done.3 = f32[512,4,768]{2,1,0:T(4,128)} async-done(((f32[512,4,768]{2,1,0:T(4,128)}), f32[512,4,768]{2,1,0:T(4,128)}, u32[]{:S(2)}, u32[]{:S(2)}) %all-to-all-start.3) | async-done | bytes 6291488 | tf_op jit(solution)/shard_map/all_to_all | solution.py:149
  792.0 15.1 %fusion.134 = f32[128,32,768]{2,0,1:T(8,128)} fusion(f32[32,64,768]{2,1,0:T(8,128)} %all_to_all.57, f32[64]{0:T(128)S(1)} %fusion.172), kind=kOutput, calls=%fused_computation.149 | convolution fusion | flops 2416041984 | bytes 18874624 | tf_op jit(solution)/shard_map/rkd,lk->rld/dot_general | solution.py:32
  807.1 19.1 %fusion.262 = (f32[32,128]{1,0:T(8,128)S(1)}, f32[32,128,768]{2,1,0:T(8,128)S(1)}) fusion(f32[768]{0:T(1024)S(1)} %copy-done.16, f32[768]{0:T(1024)S(1)} %copy-done.18, f32[32,128]{1,0:T(8,128)S(1)} %copy-done.12, f32[32,128]{1,0:T(8,128)S(1)} %copy-done.10, bf16[32,128,768]{2,1,0:T(8,128)(2,1)} %param.14, f32[128,32,768]{2,0,1:T(8,128)} %fusion.134, ...), kind=kOutput, calls=%fused_computation.276 | convolution fusion | flops 2444349440 | bytes 37804288 | tf_op jit(solution)/shard_map/rkd,lk->rld/dot_general | solution.py:32
  830.8 126.3 %fusion.2.clone.6 = bf16[4096,3072]{1,0:T(8,128)(2,1)} fusion(bf16[4096,768]{1,0:T(8,128)(2,1)S(1)} %fusion.47, bf16[768,3072]{1,0:T(8,128)(2,1)} %param.23, f32[3072]{0:T(1024)S(1)} %copy-done.21), kind=kOutput, calls=%fused_computation.3.clone.clone.clone.clone.clone.1 | convolution fusion | flops 20157825024 | bytes 36188160 | tf_op jit(solution)/shard_map/dot_general | solution.py:155
  957.2 27.6 %fusion.49 = bf16[4096,768]{1,0:T(8,128)(2,1)} fusion(f32[32,128,768]{2,1,0:T(8,128)} %copy-done, bf16[3072,768]{1,0:T(8,128)(2,1)} %param.25, f32[768]{0:T(1024)S(1)} %copy-done.22, bf16[4096,3072]{1,0:T(8,128)(2,1)} %fusion.2.clone.6), kind=kOutput, calls=%fused_computation.61 | convolution fusion | flops 19336790016 | bytes 48761856 | tf_op jit(solution)/shard_map/dot_general | solution.py:158
  984.7 509.6 %all-reduce.1 = f32[32,128,768]{2,1,0:T(8,128)} all-reduce(bf16[32,128,768]{2,1,0:T(8,128)(2,1)} %bitcast.202), channel_id=1, replica_groups=mesh['groups'=2,'member'=8,'half'=2] {'member'}, use_global_device_ids=true, to_apply=%region_4.6 | all-reduce | flops 3145728 | bytes 18874368 | tf_op jit(solution)/shard_map/psum | solution.py:165
  1494.3 11.2 subtract_convert_fusion
  (115 shorter events, 205.0 us)
Async XLA Ops:
  5.2 26.0 %copy-start.9 = (f32[32,128]{1,0:T(8,128)}, f32[32,128]{1,0:T(8,128)S(1)}, u32[]{:S(2)}) copy-start(f32[32,128]{1,0:T(8,128)S(1)} %broadcast_multiply_fusion.1) | copy-start | bytes 49156
  7.6 23.6 %copy-start.11 = (f32[32,128]{1,0:T(8,128)}, f32[32,128]{1,0:T(8,128)S(1)}, u32[]{:S(2)}) copy-start(f32[32,128]{1,0:T(8,128)S(1)} %add_rsqrt_fusion) | copy-start | bytes 49156
  23.8 121.5 %all-to-all-start.1 = ((f32[32,64,768]{2,0,1:T(8,128)}), f32[32,64,768]{2,0,1:T(8,128)}, u32[]{:S(2)}, u32[]{:S(2)}) async-start(f32[32,64,768]{2,0,1:T(8,128)} %copy.60), calls=%async_computation.1 | async-start | bytes 12582912 | tf_op jit(solution)/shard_map/all_to_all | solution.py:142
  49.6 124.2 %copy-start.13 = (f32[2,8,96]{2,1,0:T(8,128)S(1)}, f32[2,8,96]{2,1,0:T(8,128)}, u32[]{:S(2)}) copy-start(f32[2,8,96]{2,1,0:T(8,128)} %param.18) | copy-start | bytes 18436
  49.6 124.3 %copy-start.14 = (f32[2,8,96]{2,1,0:T(8,128)S(1)}, f32[2,8,96]{2,1,0:T(8,128)}, u32[]{:S(2)}) copy-start(f32[2,8,96]{2,1,0:T(8,128)} %param.20) | copy-start | bytes 18436
  145.3 142.6 %all-to-all-start = ((f32[32,64,768]{2,0,1:T(8,128)}), f32[32,64,768]{2,0,1:T(8,128)}, u32[]{:S(2)}, u32[]{:S(2)}) async-start(f32[32,64,768]{2,0,1:T(8,128)} %copy.57), calls=%async_computation | async-start | bytes 12582912 | tf_op jit(solution)/shard_map/all_to_all | solution.py:141
  193.1 101.2 %slice-start.10 = ((s8[6291456]{0:T(1024)(128)(4,1)}), s8[2097152]{0:T(1024)(128)(4,1)S(1)}, s32[]{:S(2)}) async-start(s8[6291456]{0:T(1024)(128)(4,1)} %bitcast.200), calls=%async_computation.14 | async-start | bytes 4194304
  302.2 9.9 copy-start.5
  312.1 13.8 copy-start.1
  312.1 23.6 %slice-start.4 = ((s8[6291456]{0:T(1024)(128)(4,1)}), s8[4194304]{0:T(1024)(128)(4,1)S(1)}, s32[]{:S(2)}) async-start(s8[6291456]{0:T(1024)(128)(4,1)} %bitcast.189), calls=%async_computation.8 | async-start | bytes 8388608
  312.1 23.6 %slice-start.8 = ((s8[6291456]{0:T(1024)(128)(4,1)}), s8[4194304]{0:T(1024)(128)(4,1)S(1)}, s32[]{:S(2)}) async-start(s8[6291456]{0:T(1024)(128)(4,1)} %bitcast.198), calls=%async_computation.12 | async-start | bytes 8388608
  353.8 13.2 copy-start.6
  367.0 19.4 %slice-start = ((s8[8388608]{0:T(1024)(128)(4,1)}), s8[4194304]{0:T(1024)(128)(4,1)S(1)}, s32[]{:S(2)}) async-start(s8[8388608]{0:T(1024)(128)(4,1)} %bitcast.182), calls=%async_computation.4 | async-start | bytes 8388608
  367.0 19.4 %slice-start.6 = ((s8[8388608]{0:T(1024)(128)(4,1)}), s8[4194304]{0:T(1024)(128)(4,1)S(1)}, s32[]{:S(2)}) async-start(s8[8388608]{0:T(1024)(128)(4,1)} %bitcast.192), calls=%async_computation.10 | async-start | bytes 8388608
  376.5 9.9 slice-start.7
  396.0 14.9 copy-start.2
  488.4 36.9 %slice-start.2 = ((s8[6291456]{0:T(1024)(128)(4,1)}), s8[2097152]{0:T(1024)(128)(4,1)S(1)}, s32[]{:S(2)}) async-start(s8[6291456]{0:T(1024)(128)(4,1)} %bitcast.184), calls=%async_computation.6 | async-start | bytes 4194304
  488.4 142.3 %all-to-all-start.2 = ((f32[512,4,768]{2,1,0:T(4,128)}), f32[512,4,768]{2,1,0:T(4,128)}, u32[]{:S(2)}, u32[]{:S(2)}) async-start(f32[512,4,768]{2,1,0:T(4,128)} %copy.72), calls=%async_computation.2 | async-start | bytes 12582912 | tf_op jit(solution)/shard_map/all_to_all | solution.py:148
  630.7 142.6 %all-to-all-start.3 = ((f32[512,4,768]{2,1,0:T(4,128)}), f32[512,4,768]{2,1,0:T(4,128)}, u32[]{:S(2)}, u32[]{:S(2)}) async-start(f32[512,4,768]{2,1,0:T(4,128)} %copy.76), calls=%async_computation.3 | async-start | bytes 12582912 | tf_op jit(solution)/shard_map/all_to_all | solution.py:149
  791.9 15.1 %copy-start.10 = (f32[32,128]{1,0:T(8,128)S(1)}, f32[32,128]{1,0:T(8,128)}, u32[]{:S(2)}) copy-start(f32[32,128]{1,0:T(8,128)} %copy-done.9) | copy-start | bytes 49156
  792.0 15.1 %copy-start.12 = (f32[32,128]{1,0:T(8,128)S(1)}, f32[32,128]{1,0:T(8,128)}, u32[]{:S(2)}) copy-start(f32[32,128]{1,0:T(8,128)} %copy-done.11) | copy-start | bytes 49156
  792.0 15.1 %copy-start.16 = (f32[768]{0:T(1024)S(1)}, f32[768]{0:T(1024)}, u32[]{:S(2)}) copy-start(f32[768]{0:T(1024)} %param.16) | copy-start | bytes 9220
  792.0 15.1 %copy-start.18 = (f32[768]{0:T(1024)S(1)}, f32[768]{0:T(1024)}, u32[]{:S(2)}) copy-start(f32[768]{0:T(1024)} %param.15) | copy-start | bytes 9220
  830.8 126.3 %copy-start.22 = (f32[768]{0:T(1024)S(1)}, f32[768]{0:T(1024)}, u32[]{:S(2)}) copy-start(f32[768]{0:T(1024)} %param.26) | copy-start | bytes 9220
  (15 other events, 95.8 us)
where the time goes:
time: 1520 us; the launch traced here: 1510 us
  blocking collectives  510 us (34%)
  waiting for transfers between devices  378 us (25%)
  matrix products  367 us (24%)
  local copies, waits for them, and re-layouts  136 us (9%)
  starting transfers between devices  92.8 us (6%)
  other arithmetic  21.4 us (1%)
    psum x1, blocking collectives, ensemble_step(): summed = lax.psum(state_values, 'member')  510 us
    dot_general x1, matrix products, on_device(): jnp.dot(normed2, fc1_weight, preferred_element_type=jnp.float32) + fc1_bias  126 us
    dot_general x12, matrix products, contract(): return jnp.einsum(form, left, right, precision=FULL_PRECISION)  120 us
    all_to_all x1, waiting for transfers between devices, on_device(): lax.all_to_all(imag_part, 'spatial', split_axis=1, concat_axis=0, tiled=T...  95.7 us
    all_to_all x1, waiting for transfers between devices, on_device(): lax.all_to_all(imag_part, 'spatial', split_axis=0, concat_axis=1, tiled=T...  95.6 us
    all_to_all x1, waiting for transfers between devices, on_device(): lax.all_to_all(real_part, 'spatial', split_axis=1, concat_axis=0, tiled=T...  94.8 us
    dot_general x8, matrix products, block_product(): jnp.einsum('...bi,bio->...bo', values, weight, precision=FULL_PRECISION)  92.8 us
    all_to_all x1, waiting for transfers between devices, on_device(): lax.all_to_all(real_part, 'spatial', split_axis=0, concat_axis=1, tiled=T...  91.6 us
  transfers between devices with their start and end apart: 4, of which 4 were waited for; matrix products, arithmetic and copies ran while one was open for 5% of the time, Pallas kernels for 0%

commit v1 on v0

--- a/solution.py
+++ b/solution.py
@@ -8,6 +8,18 @@
 EPSILON = 1e-06
 SHRINK = 0.01
 FULL_PRECISION = lax.Precision.HIGHEST
+
+
+def rotated_exchange(x, axis, split, join):
+    ways, here = (lax.axis_size(axis), lax.axis_index(axis))
+    width = x.shape[split] // ways
+    turned = jnp.roll(x, -here * width, axis=split)
+    got = [lax.slice_in_dim(turned, 0, width, axis=split)]
+    for far in range(1, ways):
+        sent = lax.slice_in_dim(turned, far * width, (far + 1) * width, axis=split)
+        got.append(lax.ppermute(sent, axis, [(d, (d + far) % ways) for d in range(ways)]))
+    line = jnp.concatenate(got[::-1], axis=join)
+    return jnp.roll(line, (here + 1) * got[0].shape[join], axis=join)
 
 
 def from_behind(block, axis, distance):
@@ -145,7 +157,7 @@
         real_part, imag_part, spectral_w1, spectral_b1, spectral_w2, spectral_b2
     )
     real_part, imag_part = (
-        lax.all_to_all(real_part, "spatial", split_axis=0, concat_axis=1, tiled=True),
+        rotated_exchange(real_part, "spatial", 0, 1),
         lax.all_to_all(imag_part, "spatial", split_axis=0, concat_axis=1, tiled=True),
     )
     filtered = longitude_inverse(real_part, imag_part, lon_len)

time: 1520 us -> 1560 us (1.026)
  starting transfers between devices: 92.8 us -> 196 us
  waiting for transfers between devices: 378 us -> 305 us
  blocking collectives: 510 us -> 484 us
  local copies, waits for them, and re-layouts: 136 us -> 160 us
    ppermute x0 -> x15, starting transfers between devices: none -> 132 us  [rotated_exchange(): lax.ppermute(sent, axis, [(d, (d + far) % ways) for d in range(ways)])]
    ppermute x0 -> x15, waiting for transfers between devices: none -> 114 us  [rotated_exchange(): lax.ppermute(sent, axis, [(d, (d + far) % ways) for d in range(ways)])]
    all_to_all x1, waiting for transfers between devices: 95.6 us -> 0.01 us  [on_device(): lax.all_to_all(imag_part, 'spatial', split_axis=0, concat_axis=1, tiled=T...]
    all_to_all x1 -> x0, waiting for transfers between devices: 91.6 us -> none  [on_device(): lax.all_to_all(real_part, 'spatial', split_axis=0, concat_axis=1, tiled=T...]
    concatenate x0 -> x1, local copies, waits for them, and re-layouts: none -> 37.9 us  [rotated_exchange(): return jnp.roll(line, (here + 1) * got[0].shape[join], axis=join)]
    all_to_all x1 -> x0, starting transfers between devices: 28.2 us -> none  [on_device(): lax.all_to_all(real_part, 'spatial', split_axis=0, concat_axis=1, tiled=T...]
    psum x1, blocking collectives: 510 us -> 484 us  [ensemble_step(): summed = lax.psum(state_values, 'member')]
    all_to_all x3 -> x0, local copies, waits for them, and re-layouts: 18.4 us -> none  [on_device(): lax.all_to_all(real_part, 'spatial', split_axis=0, concat_axis=1, tiled=T...]
  transfers between devices with their start and end apart: 4 -> 18, of which waited for: 4 -> 8; matrix products, arithmetic and copies ran while one was open for 5% -> 7% of each run, Pallas kernels for 0% -> 0%
where the time goes in v1:
time: 1560 us; the launch traced here: 1550 us
  blocking collectives  484 us (31%)
  matrix products  366 us (23%)
  waiting for transfers between devices  305 us (20%)
  starting transfers between devices  196 us (13%)
  local copies, waits for them, and re-layouts  160 us (10%)
  other arithmetic  36 us (2%)
    psum x1, blocking collectives, ensemble_step(): summed = lax.psum(state_values, 'member')  484 us
    ppermute x15, starting transfers between devices, rotated_exchange(): lax.ppermute(sent, axis, [(d, (d + far) % ways) for d in range(ways)])  132 us
    dot_general x1, matrix products, on_device(): jnp.dot(normed2, fc1_weight, preferred_element_type=jnp.float32) + fc1_bias  127 us
    dot_general x12, matrix products, contract(): return jnp.einsum(form, left, right, precision=FULL_PRECISION)  121 us
    ppermute x15, waiting for transfers between devices, rotated_exchange(): lax.ppermute(sent, axis, [(d, (d + far) % ways) for d in range(ways)])  114 us
    all_to_all x1, waiting for transfers between devices, on_device(): lax.all_to_all(imag_part, 'spatial', split_axis=1, concat_axis=0, tiled=T...  95.7 us
    all_to_all x1, waiting for transfers between devices, on_device(): lax.all_to_all(real_part, 'spatial', split_axis=1, concat_axis=0, tiled=T...  94.7 us
    dot_general x8, matrix products, block_product(): jnp.einsum('...bi,bio->...bo', values, weight, precision=FULL_PRECISION)  92.9 us
  transfers between devices with their start and end apart: 18, of which 8 were waited for; matrix products, arithmetic and copies ran while one was open for 7% of the time, Pallas kernels for 0%

profile of v1, /device:TPU:0, one launch (start us, length us, event | category | flops | bytes accessed | tf_op | source)
XLA Modules:
  0.0 1548.4 jit_solution(3744095920029236945)
XLA Ops:
  31.3 12.0 fusion.99
  49.6 95.7 %all-to-all-done.1 = f32[32,64,768]{2,0,1:T(8,128)} async-done(((f32[32,64,768]{2,0,1:T(8,128)}), f32[32,64,768]{2,0,1:T(8,128)}, u32[]{:S(2)}, u32[]{:S(2)}) %all-to-all-start.1) | async-done | bytes 6291488 | tf_op jit(solution)/shard_map/all_to_all | solution.py:154
  145.3 28.5 %all-to-all-start = ((f32[32,64,768]{2,0,1:T(8,128)}), f32[32,64,768]{2,0,1:T(8,128)}, u32[]{:S(2)}, u32[]{:S(2)}) async-start(f32[32,64,768]{2,0,1:T(8,128)} %copy.57), calls=%async_computation | async-start | bytes 12582912 | tf_op jit(solution)/shard_map/all_to_all | solution.py:153
  193.2 94.7 %all-to-all-done = f32[32,64,768]{2,0,1:T(8,128)} async-done(((f32[32,64,768]{2,0,1:T(8,128)}), f32[32,64,768]{2,0,1:T(8,128)}, u32[]{:S(2)}, u32[]{:S(2)}) %all-to-all-start) | async-done | bytes 6291488 | tf_op jit(solution)/shard_map/all_to_all | solution.py:153
  312.2 13.7 fusion.58
  353.9 13.1 add_maximum_fusion
  395.9 14.9 select_bitcast_fusion
  410.9 11.0 copy.70
  431.5 12.4 select_bitcast_fusion.1
  443.9 11.0 copy.69
  486.9 28.1 %all-to-all-start.2 = ((f32[512,4,768]{2,1,0:T(4,128)}), f32[512,4,768]{2,1,0:T(4,128)}, u32[]{:S(2)}, u32[]{:S(2)}) async-start(f32[512,4,768]{2,1,0:T(4,128)} %copy.75), calls=%async_computation.2 | async-start | bytes 12582912 | tf_op jit(solution)/shard_map/all_to_all | solution.py:161
  555.8 74.2 %collective-permute-done.14 = f32[32,4,768]{2,1,0:T(4,128)S(1)} collective-permute-done((f32[32,4,768]{2,1,0:T(4,128)S(1)}, f32[32,4,768]{2,1,0:T(4,128)S(1)}, u32[]{:S(2)}, u32[]{:S(2)}) %collective-permute-start.14) | collective-permute-done | bytes 393248 | tf_op jit(solution)/shard_map/ppermute | solution.py:20
  631.2 63.5 %collective-permute-start.8 = (f32[32,4,768]{2,1,0:T(4,128)S(1)}, f32[32,4,768]{2,1,0:T(4,128)S(1)}, u32[]{:S(2)}, u32[]{:S(2)}) collective-permute-start(f32[32,4,768]{2,1,0:T(4,128)S(1)} %get-tuple-element.10), channel_id=1, source_target_pairs={{0,7},{1,8},{2,9},{3,10},{4,11},{5,12},{6,13},{7,14},{8,15},{9,0},... | collective-permute-start | bytes 1179656 | tf_op jit(solution)/shard_map/ppermute | solution.py:20
  697.5 28.4 %collective-permute-done.10 = f32[32,4,768]{2,1,0:T(4,128)S(1)} collective-permute-done((f32[32,4,768]{2,1,0:T(4,128)S(1)}, f32[32,4,768]{2,1,0:T(4,128)S(1)}, u32[]{:S(2)}, u32[]{:S(2)}) %collective-permute-start.10) | collective-permute-done | bytes 393248 | tf_op jit(solution)/shard_map/ppermute | solution.py:20
  737.9 22.4 %collective-permute-start.3 = (f32[32,4,768]{2,1,0:T(4,128)}, f32[32,4,768]{2,1,0:T(4,128)}, u32[]{:S(2)}, u32[]{:S(2)}) collective-permute-start(f32[32,4,768]{2,1,0:T(4,128)} %get-tuple-element.15), channel_id=1, source_target_pairs={{0,12},{1,13},{2,14},{3,15},{4,0},{5,1},{6,2},{7,3},{8,4},{9,5},{1... | collective-permute-start | bytes 1179656 | tf_op jit(solution)/shard_map/ppermute | solution.py:20
  761.6 13.3 collective-permute-start.1
  774.9 11.8 collective-permute-start
  795.9 37.9 %concatenate.11 = f32[32,128,768]{2,1,0:T(8,128)} concatenate(f32[32,4,768]{2,1,0:T(4,128)} %collective-permute-done, f32[32,4,768]{2,1,0:T(4,128)} %collective-permute-done.1, f32[32,4,768]{2,1,0:T(4,128)} %collective-permute-done.2, f32[32,4,768]{2,1,0:T(4,128)} %collective-permute-done.3, f32[32,4,768]{2,1,0:T(4,128)} %collective-permute-done.4, ...), dimensions={1} | concatenate | bytes 25165824 | tf_op jit(solution)/shard_map/jit(_roll_dynamic)/concatenate | solution.py:22
  852.4 15.5 %fusion.126 = f32[128,32,768]{2,0,1:T(8,128)} fusion(f32[32,64,768]{2,1,0:T(8,128)} %all_to_all.44, f32[64]{0:T(128)S(1)} %fusion.189), kind=kOutput, calls=%fused_computation.141 | convolution fusion | flops 2416041984 | bytes 18874624 | tf_op jit(solution)/shard_map/rkd,lk->rld/dot_general | solution.py:44
  868.0 21.3 %fusion.268 = (f32[32,128]{1,0:T(8,128)S(1)}, f32[32,128,768]{2,1,0:T(8,128)}) fusion(f32[768]{0:T(1024)S(1)} %copy-done.18, f32[768]{0:T(1024)S(1)} %copy-done.20, f32[32,128]{1,0:T(8,128)S(1)} %copy-done.14, f32[32,128]{1,0:T(8,128)S(1)} %copy-done.12, bf16[32,128,768]{2,1,0:T(8,128)(2,1)S(1)} %bitcast.181, f32[128,32,768]{2,0,1:T(8,128)} %fusion.126, ...), kind=kOutput, calls=%fused_computation.282 | convolution fusion | flops 2444349440 | bytes 37804292 | tf_op jit(solution)/shard_map/rkd,lk->rld/dot_general | solution.py:44
  899.9 126.6 %fusion.2.clone.6 = bf16[4096,3072]{1,0:T(8,128)(2,1)} fusion(bf16[4096,768]{1,0:T(8,128)(2,1)S(1)} %fusion.47, bf16[768,3072]{1,0:T(8,128)(2,1)} %param.23, f32[3072]{0:T(1024)S(1)} %copy-done.23), kind=kOutput, calls=%fused_computation.3.clone.clone.clone.clone.clone.1 | convolution fusion | flops 20157825024 | bytes 36188160 | tf_op jit(solution)/shard_map/dot_general | solution.py:167
  1026.5 25.9 %fusion.49 = bf16[4096,768]{1,0:T(8,128)(2,1)} fusion(f32[32,128,768]{2,1,0:T(8,128)S(1)} %copy-done.1, bf16[3072,768]{1,0:T(8,128)(2,1)} %param.25, f32[768]{0:T(1024)S(1)} %copy-done.24, bf16[4096,3072]{1,0:T(8,128)(2,1)} %fusion.2.clone.6), kind=kOutput, calls=%fused_computation.63 | convolution fusion | flops 19336790016 | bytes 48761856 | tf_op jit(solution)/shard_map/dot_general | solution.py:170
  1052.5 484.2 %all-reduce.1 = f32[32,128,768]{2,1,0:T(8,128)} all-reduce(bf16[32,128,768]{2,1,0:T(8,128)(2,1)} %bitcast.199), channel_id=1, replica_groups=mesh['groups'=2,'member'=8,'half'=2] {'member'}, use_global_device_ids=true, to_apply=%region_4.6 | all-reduce | flops 3145728 | bytes 18874368 | tf_op jit(solution)/shard_map/psum | solution.py:177
  1536.7 11.2 subtract_convert_fusion
  (152 shorter events, 275.3 us)
Async XLA Ops:
  5.2 26.0 %copy-start.11 = (f32[32,128]{1,0:T(8,128)}, f32[32,128]{1,0:T(8,128)S(1)}, u32[]{:S(2)}) copy-start(f32[32,128]{1,0:T(8,128)S(1)} %broadcast_multiply_fusion.1) | copy-start | bytes 49156
  23.8 121.5 %all-to-all-start.1 = ((f32[32,64,768]{2,0,1:T(8,128)}), f32[32,64,768]{2,0,1:T(8,128)}, u32[]{:S(2)}, u32[]{:S(2)}) async-start(f32[32,64,768]{2,0,1:T(8,128)} %copy.60), calls=%async_computation.1 | async-start | bytes 12582912 | tf_op jit(solution)/shard_map/all_to_all | solution.py:154
  49.6 124.2 %copy-start.15 = (f32[2,8,96]{2,1,0:T(8,128)S(1)}, f32[2,8,96]{2,1,0:T(8,128)}, u32[]{:S(2)}) copy-start(f32[2,8,96]{2,1,0:T(8,128)} %param.18) | copy-start | bytes 18436
  49.6 124.3 %copy-start.16 = (f32[2,8,96]{2,1,0:T(8,128)S(1)}, f32[2,8,96]{2,1,0:T(8,128)}, u32[]{:S(2)}) copy-start(f32[2,8,96]{2,1,0:T(8,128)} %param.20) | copy-start | bytes 18436
  145.3 142.6 %all-to-all-start = ((f32[32,64,768]{2,0,1:T(8,128)}), f32[32,64,768]{2,0,1:T(8,128)}, u32[]{:S(2)}, u32[]{:S(2)}) async-start(f32[32,64,768]{2,0,1:T(8,128)} %copy.57), calls=%async_computation | async-start | bytes 12582912 | tf_op jit(solution)/shard_map/all_to_all | solution.py:153
  193.2 101.1 %slice-start.12 = ((s8[6291456]{0:T(1024)(128)(4,1)}), s8[2097152]{0:T(1024)(128)(4,1)S(1)}, s32[]{:S(2)}) async-start(s8[6291456]{0:T(1024)(128)(4,1)} %bitcast.197), calls=%async_computation.15 | async-start | bytes 4194304
  486.9 346.9 %all-to-all-start.2 = ((f32[512,4,768]{2,1,0:T(4,128)}), f32[512,4,768]{2,1,0:T(4,128)}, u32[]{:S(2)}, u32[]{:S(2)}) async-start(f32[512,4,768]{2,1,0:T(4,128)} %copy.75), calls=%async_computation.2 | async-start | bytes 12582912 | tf_op jit(solution)/shard_map/all_to_all | solution.py:161
  550.0 80.1 %collective-permute-start.14 = (f32[32,4,768]{2,1,0:T(4,128)S(1)}, f32[32,4,768]{2,1,0:T(4,128)S(1)}, u32[]{:S(2)}, u32[]{:S(2)}) collective-permute-start(f32[32,4,768]{2,1,0:T(4,128)S(1)} %get-tuple-element.4), channel_id=1, source_target_pairs={{0,1},{1,2},{2,3},{3,4},{4,5},{5,6},{6,7},{7,8},{8,9},{9,10},{10,1... | collective-permute-start | bytes 1179656 | tf_op jit(solution)/shard_map/ppermute | solution.py:20
  550.3 81.0 %collective-permute-start.13 = (f32[32,4,768]{2,1,0:T(4,128)S(1)}, f32[32,4,768]{2,1,0:T(4,128)S(1)}, u32[]{:S(2)}, u32[]{:S(2)}) collective-permute-start(f32[32,4,768]{2,1,0:T(4,128)S(1)} %get-tuple-element.5), channel_id=1, source_target_pairs={{0,2},{1,3},{2,4},{3,5},{4,6},{5,7},{6,8},{7,9},{8,10},{9,11},{10,... | collective-permute-start | bytes 1179656 | tf_op jit(solution)/shard_map/ppermute | solution.py:20
  552.0 142.7 %collective-permute-start.12 = (f32[32,4,768]{2,1,0:T(4,128)S(1)}, f32[32,4,768]{2,1,0:T(4,128)S(1)}, u32[]{:S(2)}, u32[]{:S(2)}) collective-permute-start(f32[32,4,768]{2,1,0:T(4,128)S(1)} %get-tuple-element.6), channel_id=1, source_target_pairs={{0,3},{1,4},{2,5},{3,6},{4,7},{5,8},{6,9},{7,10},{8,11},{9,12},{10... | collective-permute-start | bytes 1179656 | tf_op jit(solution)/shard_map/ppermute | solution.py:20
  554.3 140.4 %collective-permute-start.11 = (f32[32,4,768]{2,1,0:T(4,128)S(1)}, f32[32,4,768]{2,1,0:T(4,128)S(1)}, u32[]{:S(2)}, u32[]{:S(2)}) collective-permute-start(f32[32,4,768]{2,1,0:T(4,128)S(1)} %get-tuple-element.7), channel_id=1, source_target_pairs={{0,4},{1,5},{2,6},{3,7},{4,8},{5,9},{6,10},{7,11},{8,12},{9,13},{1... | collective-permute-start | bytes 1179656 | tf_op jit(solution)/shard_map/ppermute | solution.py:20
  555.7 170.2 %collective-permute-start.10 = (f32[32,4,768]{2,1,0:T(4,128)S(1)}, f32[32,4,768]{2,1,0:T(4,128)S(1)}, u32[]{:S(2)}, u32[]{:S(2)}) collective-permute-start(f32[32,4,768]{2,1,0:T(4,128)S(1)} %get-tuple-element.8), channel_id=1, source_target_pairs={{0,5},{1,6},{2,7},{3,8},{4,9},{5,10},{6,11},{7,12},{8,13},{9,14},{... | collective-permute-start | bytes 1179656 | tf_op jit(solution)/shard_map/ppermute | solution.py:20
  630.1 97.1 %collective-permute-start.9 = (f32[32,4,768]{2,1,0:T(4,128)S(1)}, f32[32,4,768]{2,1,0:T(4,128)S(1)}, u32[]{:S(2)}, u32[]{:S(2)}) collective-permute-start(f32[32,4,768]{2,1,0:T(4,128)S(1)} %get-tuple-element.9), channel_id=1, source_target_pairs={{0,6},{1,7},{2,8},{3,9},{4,10},{5,11},{6,12},{7,13},{8,14},{9,15},... | collective-permute-start | bytes 1179656 | tf_op jit(solution)/shard_map/ppermute | solution.py:20
  631.2 106.7 %collective-permute-start.8 = (f32[32,4,768]{2,1,0:T(4,128)S(1)}, f32[32,4,768]{2,1,0:T(4,128)S(1)}, u32[]{:S(2)}, u32[]{:S(2)}) collective-permute-start(f32[32,4,768]{2,1,0:T(4,128)S(1)} %get-tuple-element.10), channel_id=1, source_target_pairs={{0,7},{1,8},{2,9},{3,10},{4,11},{5,12},{6,13},{7,14},{8,15},{9,0},... | collective-permute-start | bytes 1179656 | tf_op jit(solution)/shard_map/ppermute | solution.py:20
  694.7 65.6 %collective-permute-start.7 = (f32[32,4,768]{2,1,0:T(4,128)S(1)}, f32[32,4,768]{2,1,0:T(4,128)}, u32[]{:S(2)}, u32[]{:S(2)}) collective-permute-start(f32[32,4,768]{2,1,0:T(4,128)S(1)} %get-tuple-element.11), channel_id=1, source_target_pairs={{0,8},{1,9},{2,10},{3,11},{4,12},{5,13},{6,14},{7,15},{8,0},{9,1},... | collective-permute-start | bytes 1179656 | tf_op jit(solution)/shard_map/ppermute | solution.py:20
  694.7 66.9 %collective-permute-start.6 = (f32[32,4,768]{2,1,0:T(4,128)S(1)}, f32[32,4,768]{2,1,0:T(4,128)}, u32[]{:S(2)}, u32[]{:S(2)}) collective-permute-start(f32[32,4,768]{2,1,0:T(4,128)S(1)} %get-tuple-element.12), channel_id=1, source_target_pairs={{0,9},{1,10},{2,11},{3,12},{4,13},{5,14},{6,15},{7,0},{8,1},{9,2},... | collective-permute-start | bytes 1179656 | tf_op jit(solution)/shard_map/ppermute | solution.py:20
  725.9 49.0 %collective-permute-start.5 = (f32[32,4,768]{2,1,0:T(4,128)S(1)}, f32[32,4,768]{2,1,0:T(4,128)}, u32[]{:S(2)}, u32[]{:S(2)}) collective-permute-start(f32[32,4,768]{2,1,0:T(4,128)S(1)} %get-tuple-element.13), channel_id=1, source_target_pairs={{0,10},{1,11},{2,12},{3,13},{4,14},{5,15},{6,0},{7,1},{8,2},{9,3},... | collective-permute-start | bytes 1179656 | tf_op jit(solution)/shard_map/ppermute | solution.py:20
  727.1 59.6 %collective-permute-start.4 = (f32[32,4,768]{2,1,0:T(4,128)}, f32[32,4,768]{2,1,0:T(4,128)}, u32[]{:S(2)}, u32[]{:S(2)}) collective-permute-start(f32[32,4,768]{2,1,0:T(4,128)} %get-tuple-element.14), channel_id=1, source_target_pairs={{0,11},{1,12},{2,13},{3,14},{4,15},{5,0},{6,1},{7,2},{8,3},{9,4},{... | collective-permute-start | bytes 1179656 | tf_op jit(solution)/shard_map/ppermute | solution.py:20
  737.9 48.8 %collective-permute-start.3 = (f32[32,4,768]{2,1,0:T(4,128)}, f32[32,4,768]{2,1,0:T(4,128)}, u32[]{:S(2)}, u32[]{:S(2)}) collective-permute-start(f32[32,4,768]{2,1,0:T(4,128)} %get-tuple-element.15), channel_id=1, source_target_pairs={{0,12},{1,13},{2,14},{3,15},{4,0},{5,1},{6,2},{7,3},{8,4},{9,5},{1... | collective-permute-start | bytes 1179656 | tf_op jit(solution)/shard_map/ppermute | solution.py:20
  760.3 26.4 %collective-permute-start.2 = (f32[32,4,768]{2,1,0:T(4,128)}, f32[32,4,768]{2,1,0:T(4,128)}, u32[]{:S(2)}, u32[]{:S(2)}) collective-permute-start(f32[32,4,768]{2,1,0:T(4,128)} %get-tuple-element.16), channel_id=1, source_target_pairs={{0,13},{1,14},{2,15},{3,0},{4,1},{5,2},{6,3},{7,4},{8,5},{9,6},{10... | collective-permute-start | bytes 1179656 | tf_op jit(solution)/shard_map/ppermute | solution.py:20
  761.6 31.2 %collective-permute-start.1 = (f32[32,4,768]{2,1,0:T(4,128)}, f32[32,4,768]{2,1,0:T(4,128)}, u32[]{:S(2)}, u32[]{:S(2)}) collective-permute-start(f32[32,4,768]{2,1,0:T(4,128)} %get-tuple-element.17), channel_id=1, source_target_pairs={{0,14},{1,15},{2,0},{3,1},{4,2},{5,3},{6,4},{7,5},{8,6},{9,7},{10,... | collective-permute-start | bytes 1179656 | tf_op jit(solution)/shard_map/ppermute | solution.py:20
  774.9 21.0 %collective-permute-start = (f32[32,4,768]{2,1,0:T(4,128)}, f32[32,4,768]{2,1,0:T(4,128)}, u32[]{:S(2)}, u32[]{:S(2)}) collective-permute-start(f32[32,4,768]{2,1,0:T(4,128)} %get-tuple-element.18), channel_id=1, source_target_pairs={{0,15},{1,0},{2,1},{3,2},{4,3},{5,4},{6,5},{7,6},{8,7},{9,8},{10,9... | collective-permute-start | bytes 1179656 | tf_op jit(solution)/shard_map/ppermute | solution.py:20
  899.9 126.6 %copy-start.1 = (f32[32,128,768]{2,1,0:T(8,128)S(1)}, f32[32,128,768]{2,1,0:T(8,128)}, u32[]{:S(2)}) copy-start(f32[32,128,768]{2,1,0:T(8,128)} %get-tuple-element.26) | copy-start | bytes 37748740
  899.9 126.6 %copy-start.24 = (f32[768]{0:T(1024)S(1)}, f32[768]{0:T(1024)}, u32[]{:S(2)}) copy-start(f32[768]{0:T(1024)} %param.26) | copy-start | bytes 9220
  (33 other events, 401.4 us)
